TPU v7x, 512 devices: a whole 4x4x16 slice. The times are simulated.
512 devices in a mesh: dp: 2 (over y_lo), tensor: 4 (over x), context: 64 (over z, y_hi, core).
Axes of the slice: x: 4, y: 4 (y_hi: 2, y_lo: 2; y = y_hi * 2 + y_lo), z: 16, core: 2. Of those that a mesh axis runs over, the one named last changes fastest.
Arguments:
- q_in: bfloat16 [2, 8192, 4096], P('dp', 'context', 'tensor'), may hold values from -44 to 44
- k_in: bfloat16 [2, 8192, 4096], P('dp', 'context', 'tensor'), may hold values from -6 to 6
- v_in: bfloat16 [2, 8192, 4096], P('dp', 'context', 'tensor'), may hold values from -6 to 6
- short_filt: float32 [3, 7, 4096], P(None, None, 'tensor'), may hold values from -2 to 2
- long_filt: float32 [8192, 4096], P('context', 'tensor'), may hold values from -1.1 to 1.1
- norm_gain: float32 [4096], P('tensor'), may hold values from 0.1 to 1.9
- grad_out: bfloat16 [2, 8192, 4096], P('dp', 'context', 'tensor'), may hold values from -6 to 6
Outputs:
- mixed: bfloat16 [2, 8192, 4096], P('dp', 'context', 'tensor')
- grad_inputs: bfloat16 [3, 2, 8192, 4096], P(None, 'dp', 'context', 'tensor')
- grad_long: float32 [8192, 4096], P('context', 'tensor')
- grad_short: float32 [3, 7, 4096], P(None, None, 'tensor')
All inputs are finite; a program needn't handle non-finite values.
Results may differ from a plain program's by a relative error of at most 0.00225.
Values may be sent and summed in bfloat16 or wider, within the bound.
No kernel may reach another device: no remote copies, remote signals or barrier semaphores. Data moves between devices by JAX's collectives and lax.ppermute only.
A program may use at most 128 MiB of HBM per device.

v0:
```python
import math
import jax
import jax.numpy as jnp
from jax import lax
from jax.sharding import PartitionSpec as P

D = 4096
FILT = 7
EPS = 1e-06
HIGH = lax.Precision.HIGHEST


def passed_along(shard, axis, by):
    peers = lax.axis_size(axis)
    pairs = [(i, i + by) for i in range(peers) if 0 <= i + by < peers]
    return lax.ppermute(shard, axis, pairs)


def phases(first, second, modulus):
    product = first[:, None] * second[None, :] % modulus
    return product.astype(jnp.float32) * (2.0 * math.pi / modulus)


def block_table(block_len, sign):
    index = jnp.arange(block_len, dtype=jnp.int32)
    angle = phases(index, index, block_len)
    cosine = jnp.cos(angle)
    sine = jnp.sin(angle) * sign
    return jnp.stack([jnp.stack([cosine, sine]), jnp.stack([-sine, cosine])])


def forward_rows(values, modulus):
    count, block_len, width = values.shape
    ctx_size = lax.axis_size("context")
    sub_len = block_len // ctx_size
    spread = lax.all_to_all(
        values.reshape(count, 1, block_len, width),
        "context",
        split_axis=2,
        concat_axis=1,
        tiled=True,
    )
    freq = jnp.arange(2 * ctx_size, dtype=jnp.int32)
    place = (
        jnp.arange(ctx_size, dtype=jnp.int32)[:, None] * block_len
        + lax.axis_index("context") * sub_len
        + jnp.arange(sub_len, dtype=jnp.int32)[None, :]
    )
    angle = (freq[:, None, None] * place[None] % modulus).astype(jnp.float32) * (
        2.0 * math.pi / modulus
    )
    table = jnp.stack([jnp.cos(angle), -jnp.sin(angle)])
    turned = jnp.einsum("pkcs,ncsx->npksx", table, spread, precision=HIGH)
    moved = lax.all_to_all(turned, "context", split_axis=2, concat_axis=3, tiled=True)
    return jnp.einsum("pqmb,nqjbx->npjmx", block_table(block_len, 1.0), moved, precision=HIGH)


def inverse_rows(spec, modulus):
    rows = spec.shape[2]
    block_len = spec.shape[3]
    ctx_size = lax.axis_size("context")
    index = jnp.arange(block_len, dtype=jnp.int32)
    freq = 2 * lax.axis_index("context") + jnp.arange(rows, dtype=jnp.int32)
    total = freq[:, None, None] + 2 * ctx_size * index[None, :, None]
    angle = (total * index[None, None, :] % modulus).astype(jnp.float32) * (2.0 * math.pi / modulus)
    cosine = jnp.cos(angle)
    sine = jnp.sin(angle)
    table = jnp.stack([jnp.stack([cosine, -sine]), jnp.stack([sine, cosine])])
    turned = jnp.einsum("pqjmb,nqjmx->npjbx", table, spec, precision=HIGH)
    moved = lax.all_to_all(turned, "context", split_axis=3, concat_axis=2, tiled=True)
    outer = phases(
        jnp.arange(ctx_size, dtype=jnp.int32),
        jnp.arange(2 * ctx_size, dtype=jnp.int32),
        2 * ctx_size,
    )
    real_table = jnp.stack([jnp.cos(outer), -jnp.sin(outer)])
    values = jnp.einsum("qck,nqksx->ncsx", real_table, moved, precision=HIGH) / modulus
    back = lax.all_to_all(values, "context", split_axis=1, concat_axis=2, tiled=True)
    return back.reshape(back.shape[0], back.shape[2], back.shape[3])


def shards(q_in, k_in, v_in, short_filt, long_filt, norm_gain, grad_out):
    block_len = q_in.shape[1]
    channels = q_in.shape[2]
    edge_rows = FILT - 1
    modulus = 2 * lax.axis_size("context") * block_len
    branches = jnp.stack([q_in[0], k_in[0], v_in[0]])
    before = passed_along(branches[:, block_len - edge_rows :], "context", 1)
    inputs = jnp.concatenate([before, branches], 1).astype(jnp.float32)
    shorts = jnp.zeros((3, block_len, channels), jnp.float32)
    for lag in range(FILT):
        shorts = (
            shorts
            + short_filt[:, lag][:, None, :]
            * inputs[:, edge_rows - lag : edge_rows - lag + block_len]
        )
    q_short = shorts[0]
    k_short = shorts[1]
    v_short = shorts[2]
    kv_prod = k_short * v_short
    spectra = forward_rows(jnp.stack([kv_prod, long_filt]), modulus)
    kv_real, kv_imag = (spectra[0, 0], spectra[0, 1])
    filt_real, filt_imag = (spectra[1, 0], spectra[1, 1])
    conv_spec = jnp.stack(
        [kv_real * filt_real - kv_imag * filt_imag, kv_real * filt_imag + kv_imag * filt_real]
    )[None]
    conv = inverse_rows(conv_spec, modulus)[0]
    y_out = q_short * conv
    squares = lax.psum(jnp.sum(y_out * y_out, axis=-1), "tensor")
    rms = jnp.sqrt(squares / D + EPS)[:, None]
    mixed = (y_out / rms * norm_gain).astype(jnp.bfloat16)[None]
    grad_z = grad_out[0].astype(jnp.float32) * norm_gain
    prods = lax.psum(jnp.sum(grad_z * y_out, axis=-1), "tensor")[:, None]
    grad_y = grad_z / rms - y_out * prods / (D * rms**3)
    dconv = grad_y * q_short
    grad_q = grad_y * conv
    grad_spec = forward_rows(dconv[None], modulus)[0]
    grad_real = grad_spec[0]
    grad_imag = grad_spec[1]
    dkv_spec = jnp.stack(
        [
            filt_real * grad_real + filt_imag * grad_imag,
            filt_real * grad_imag - filt_imag * grad_real,
        ]
    )
    dfilt_spec = jnp.stack(
        [kv_real * grad_real + kv_imag * grad_imag, kv_real * grad_imag - kv_imag * grad_real]
    )
    results = inverse_rows(jnp.stack([dkv_spec, dfilt_spec]), modulus)
    dkv = results[0]
    dfilt_local = results[1]
    grads = jnp.stack([grad_q, dkv * v_short, dkv * k_short])
    after = passed_along(grads[:, :edge_rows].astype(jnp.bfloat16), "context", -1).astype(
        jnp.float32
    )
    extended = jnp.concatenate([grads, after], 1)
    grad_inputs = jnp.zeros((3, block_len, channels), jnp.float32)
    for lag in range(FILT):
        grad_inputs = (
            grad_inputs + short_filt[:, lag][:, None, :] * extended[:, lag : lag + block_len]
        )
    short_local = jnp.stack(
        [
            jnp.sum(grads * inputs[:, edge_rows - lag : edge_rows - lag + block_len], axis=1)
            for lag in range(FILT)
        ],
        1,
    )
    scale = 1.0 / math.sqrt(lax.axis_size("dp") * block_len * lax.axis_size("context"))
    grad_long = lax.psum(dfilt_local, "dp") * scale
    grad_short = lax.psum(short_local, ("dp", "context")) * scale
    return (mixed, grad_inputs.astype(jnp.bfloat16)[:, None], grad_long, grad_short)


def solution(mesh):
    in_specs = (
        P("dp", "context", "tensor"),
        P("dp", "context", "tensor"),
        P("dp", "context", "tensor"),
        P(None, None, "tensor"),
        P("context", "tensor"),
        P("tensor"),
        P("dp", "context", "tensor"),
    )
    out_specs = (
        P("dp", "context", "tensor"),
        P(None, "dp", "context", "tensor"),
        P("context", "tensor"),
        P(None, None, "tensor"),
    )
    return jax.shard_map(shards, mesh=mesh, in_specs=in_specs, out_specs=out_specs, check_vma=False)
```

profile of v0, /device:TPU:1, one launch (start us, length us, event | category | flops | bytes accessed | tf_op | source)
XLA Modules:
  0.0 1352.6 jit_solution(16455876887592393104)
XLA Ops:
  7.2 1.4 copy.63
  8.6 1.4 copy.64
  10.0 1.4 copy.65
  11.4 6.2 collective-permute-start
  18.2 2.1 collective-permute-done
  20.3 1.9 maximum_convert_fusion
  22.3 3.9 multiply_add_fusion
  26.2 1.4 copy-done.2
  27.6 1.8 fusion.95
  29.3 1.9 maximum_bitcast_fusion.4
  31.3 17.8 %all-to-all-start = ((f32[2,1,128,1024]{3,0,1,2:T(2,128)}), f32[2,1,128,1024]{3,0,1,2:T(2,128)S(1)}, u32[]{:S(2)}, u32[]{:S(2)}) async-start(f32[2,1,128,1024]{3,0,1,2:T(2,128)} %maximum_bitcast_fusion.4), calls=%async_computation | async-start | bytes 2097152 | tf_op jit(solution)/shard_map/all_to_all | solution.py:36
  49.5 53.7 %all-to-all-done = f32[2,1,128,1024]{3,0,1,2:T(2,128)S(1)} async-done(((f32[2,1,128,1024]{3,0,1,2:T(2,128)}), f32[2,1,128,1024]{3,0,1,2:T(2,128)S(1)}, u32[]{:S(2)}, u32[]{:S(2)}) %all-to-all-start) | async-done | bytes 1048608 | tf_op jit(solution)/shard_map/all_to_all | solution.py:36
  103.1 5.2 convolution_bitcast_fusion
  108.3 7.3 copy.68
  115.6 7.8 all-to-all-start.1
  124.8 184.3 %all-to-all-done.1 = f32[2,2,128,2,1024]{4,1,0,3,2:T(2,128)} async-done(((f32[2,2,128,2,1024]{4,1,0,3,2:T(2,128)}), f32[2,2,128,2,1024]{4,1,0,3,2:T(2,128)}, u32[]{:S(2)}, u32[]{:S(2)}) %all-to-all-start.1) | async-done | bytes 4194336 | tf_op jit(solution)/shard_map/all_to_all | solution.py:54
  309.1 5.4 copy.70
  314.5 8.1 fusion.4
  322.9 1.7 copy-done
  324.6 3.3 fusion.21
  328.0 4.2 copy.79
  332.2 10.6 all-to-all-start.2
  343.0 98.5 %all-to-all-done.2 = f32[1,2,2,128,1024]{4,1,2,0,3:T(2,128)} async-done(((f32[1,2,2,128,1024]{4,1,2,0,3:T(2,128)}), f32[1,2,2,128,1024]{4,1,2,0,3:T(2,128)}, u32[]{:S(2)}, u32[]{:S(2)}) %all-to-all-start.2) | async-done | bytes 2097184 | tf_op jit(solution)/shard_map/all_to_all | solution.py:70
  441.4 2.7 copy.80
  444.1 2.2 copy.81
  446.3 3.7 reshape.785
  450.0 3.1 fusion.30
  454.3 7.7 all-to-all-start.3
  463.2 32.8 %all-to-all-done.3 = f32[1,64,2,1024]{3,2,0,1:T(2,128)S(1)} async-done(((f32[1,64,2,1024]{3,2,0,1:T(2,128)}), f32[1,64,2,1024]{3,2,0,1:T(2,128)S(1)}, u32[]{:S(2)}, u32[]{:S(2)}) %all-to-all-start.3) | async-done | bytes 524320 | tf_op jit(solution)/shard_map/all_to_all | solution.py:78
  497.2 2.2 fusion.44
  499.4 9.3 all-reduce
  509.9 1.6 squeeze_reshape.9
  511.5 3.0 fusion.48
  514.5 40.9 %all_to_all.105 = f32[1,1,128,1024]{3,0,1,2:T(1,128)} all-to-all(f32[1,1,128,1024]{3,0,1,2:T(1,128)S(1)} %fusion.48), channel_id=1, replica_groups=mesh['dp'=2,'tensor'=4,'context'=64] {'context'}, dimensions={2} | all-to-all | bytes 1048576 | tf_op jit(solution)/shard_map/all_to_all | solution.py:36
  555.4 3.1 reduce
  558.5 2.1 reshape.786
  560.6 4.3 convolution_bitcast_fusion.1
  564.9 4.2 copy.86
  569.1 103.5 %all_to_all.106 = f32[1,2,128,2,1024]{4,1,3,0,2:T(2,128)S(1)} all-to-all(f32[1,2,128,2,1024]{4,1,3,0,2:T(2,128)} %copy.86), channel_id=1, replica_groups=mesh['dp'=2,'tensor'=4,'context'=64] {'context'}, dimensions={2} | all-to-all | bytes 4194304 | tf_op jit(solution)/shard_map/all_to_all | solution.py:54
  673.7 2.5 copy.88
  676.2 4.1 copy.89
  680.3 3.6 fusion.24
  684.8 5.0 fusion.7
  689.7 7.3 copy.95
  697.1 196.5 %all_to_all.107 = f32[2,2,2,128,1024]{4,1,0,2,3:T(2,128)S(1)} all-to-all(f32[2,2,2,128,1024]{4,1,0,2,3:T(2,128)} %copy.95), channel_id=1, replica_groups=mesh['dp'=2,'tensor'=4,'context'=64] {'context'}, dimensions={3} | all-to-all | bytes 8388608 | tf_op jit(solution)/shard_map/all_to_all | solution.py:70
  893.6 5.3 copy.97
  898.8 6.0 all_to_all.95
  904.9 4.6 fusion.28
  909.5 1.8 copy.98
  911.2 8.2 all-to-all-start.7
  919.5 1.6 squeeze_reshape.7
  921.1 52.3 %all-to-all-done.7 = f32[2,64,2,1024]{3,2,0,1:T(2,128)} async-done(((f32[2,64,2,1024]{3,2,0,1:T(2,128)}), f32[2,64,2,1024]{3,2,0,1:T(2,128)}, u32[]{:S(2)}, u32[]{:S(2)}) %all-to-all-start.7) | async-done | bytes 1048608 | tf_op jit(solution)/shard_map/all_to_all | solution.py:78
  973.4 2.1 fusion.96
  975.5 1.6 squeeze.10
  977.1 7.5 fusion.41
  984.6 4.3 multiply_reduce_fusion
  990.1 2.5 pad_maximum_fusion.1
  992.6 4.4 collective-permute-start.1
  999.2 2.3 collective-permute-done.1
  1001.5 2.5 pad_maximum_fusion
  1004.1 3.8 fusion.40
  1009.0 289.3 %all-reduce.6.cloned.1.call-done = f32[3,7,1024]{2,0,1:T(4,128)} async-done(((f32[3,7,1024]{2,0,1:T(4,128)}), f32[3,7,1024]{2,0,1:T(4,128)}) %all-reduce.6.cloned.1.call-update) | async-done | bytes 86032 | tf_op jit(solution)/shard_map/psum | solution.py:151
  1299.9 43.4 %all-reduce.4.cloned.1.call-done = f32[128,1024]{1,0:T(8,128)} async-done(((f32[128,1024]{1,0:T(8,128)}), f32[128,1024]{1,0:T(8,128)}) %all-reduce.4.cloned.1.call-update) | async-done | bytes 524304 | tf_op jit(solution)/shard_map/psum | solution.py:150
  1343.4 1.9 broadcast_multiply_fusion
  (111 shorter events, 15.3 us)
Async XLA Ops:
  7.2 10.5 copy-start.28
  7.2 10.7 copy-start.12
  11.4 8.9 collective-permute-start
  17.7 4.5 copy-start.16
  17.8 4.4 copy-start.18
  17.8 4.4 copy-start.20
  17.8 4.4 copy-start.22
  17.8 4.4 copy-start.24
  17.9 4.4 copy-start.26
  26.2 1.4 copy-start.2
  31.3 71.9 %all-to-all-start = ((f32[2,1,128,1024]{3,0,1,2:T(2,128)}), f32[2,1,128,1024]{3,0,1,2:T(2,128)S(1)}, u32[]{:S(2)}, u32[]{:S(2)}) async-start(f32[2,1,128,1024]{3,0,1,2:T(2,128)} %maximum_bitcast_fusion.4), calls=%async_computation | async-start | bytes 2097152 | tf_op jit(solution)/shard_map/all_to_all | solution.py:36
  49.4 58.9 %copy-start.10 = (f32[1,128,64,2]{1,2,0,3:T(8,128)}, f32[1,128,64,2]{1,2,0,3:T(8,128)S(1)}, u32[]{:S(2)}) copy-start(f32[1,128,64,2]{1,2,0,3:T(8,128)S(1)} %get-tuple-element.55) | copy-start | bytes 196612
  49.5 58.9 %copy-start.11 = (f32[1,128,64,2]{1,2,0,3:T(8,128)}, f32[1,128,64,2]{1,2,0,3:T(8,128)S(1)}, u32[]{:S(2)}) copy-start(f32[1,128,64,2]{1,2,0,3:T(8,128)S(1)} %get-tuple-element.56) | copy-start | bytes 196612
  115.6 193.4 %all-to-all-start.1 = ((f32[2,2,128,2,1024]{4,1,0,3,2:T(2,128)}), f32[2,2,128,2,1024]{4,1,0,3,2:T(2,128)}, u32[]{:S(2)}, u32[]{:S(2)}) async-start(f32[2,2,128,2,1024]{4,1,0,3,2:T(2,128)} %copy.68), calls=%async_computation.1 | async-start | bytes 8388608 | tf_op jit(solution)/shard_map/all_to_all | solution.py:54
  124.0 190.5 %copy-start.8 = (f32[1,2,128,128]{3,2,1,0:T(8,128)}, f32[1,2,128,128]{3,2,1,0:T(8,128)S(1)}, u32[]{:S(2)}) copy-start(f32[1,2,128,128]{3,2,1,0:T(8,128)S(1)} %get-tuple-element.50) | copy-start | bytes 393220
  124.0 190.5 %copy-start.9 = (f32[1,2,128,128]{3,2,1,0:T(8,128)}, f32[1,2,128,128]{3,2,1,0:T(8,128)S(1)}, u32[]{:S(2)}) copy-start(f32[1,2,128,128]{3,2,1,0:T(8,128)S(1)} %get-tuple-element.51) | copy-start | bytes 393220
  322.7 2.0 copy-start
  332.2 109.2 %all-to-all-start.2 = ((f32[1,2,2,128,1024]{4,1,2,0,3:T(2,128)}), f32[1,2,2,128,1024]{4,1,2,0,3:T(2,128)}, u32[]{:S(2)}, u32[]{:S(2)}) async-start(f32[1,2,2,128,1024]{4,1,2,0,3:T(2,128)} %copy.79), calls=%async_computation.2 | async-start | bytes 4194304 | tf_op jit(solution)/shard_map/all_to_all | solution.py:70
  342.9 107.1 %copy-start.13 = (f32[1,64,128]{2,1,0:T(8,128)}, f32[1,64,128]{2,1,0:T(8,128)S(1)}, u32[]{:S(2)}) copy-start(f32[1,64,128]{2,1,0:T(8,128)S(1)} %get-tuple-element.68) | copy-start | bytes 98308
  450.0 12.0 copy-start.5
  454.3 41.7 %all-to-all-start.3 = ((f32[1,64,2,1024]{3,2,0,1:T(2,128)}), f32[1,64,2,1024]{3,2,0,1:T(2,128)S(1)}, u32[]{:S(2)}, u32[]{:S(2)}) async-start(f32[1,64,2,1024]{3,2,0,1:T(2,128)} %copy.82), calls=%async_computation.3 | async-start | bytes 1048576 | tf_op jit(solution)/shard_map/all_to_all | solution.py:78
  680.3 3.6 copy-start.1
  898.8 6.0 copy-start.14
  911.2 62.2 %all-to-all-start.7 = ((f32[2,64,2,1024]{3,2,0,1:T(2,128)}), f32[2,64,2,1024]{3,2,0,1:T(2,128)}, u32[]{:S(2)}, u32[]{:S(2)}) async-start(f32[2,64,2,1024]{3,2,0,1:T(2,128)} %copy.98), calls=%async_computation.7 | async-start | bytes 2097152 | tf_op jit(solution)/shard_map/all_to_all | solution.py:78
  919.5 57.7 %copy-start.29 = (f32[1024]{0:T(1024)S(1)}, f32[1024]{0:T(1024)}, u32[]{:S(2)}) copy-start(f32[1024]{0:T(1024)} %param.12) | copy-start | bytes 12292
  919.5 57.6 %copy-start.30 = (f32[128]{0:T(128)S(1)}, f32[128]{0:T(128)}, u32[]{:S(2)}) copy-start(f32[128]{0:T(128)} %get-tuple-element.22) | copy-start | bytes 1540
  919.5 57.6 %copy-start.31 = (f32[128]{0:T(128)S(1)}, f32[128]{0:T(128)}, u32[]{:S(2)}) copy-start(f32[128]{0:T(128)} %get-tuple-element.57) | copy-start | bytes 1540
  919.5 57.6 %copy-start.32 = (f32[128]{0:T(128)S(1)}, f32[128]{0:T(128)}, u32[]{:S(2)}) copy-start(f32[128]{0:T(128)} %get-tuple-element.58) | copy-start | bytes 1540
  919.5 378.8 %all-reduce.6.cloned.1.call-start = ((), (), s32[]{:S(2)}) async-start(), calls=%async_computation.9 | async-start | bytes 229376 | tf_op jit(solution)/shard_map/psum | solution.py:151
  984.6 4.3 copy-start.3
  989.0 8.1 copy-start.7
  989.0 9.3 copy-start.6
  989.1 0.6 copy-start.15
  989.8 353.6 %all-reduce.4.cloned.1.call-start = ((), (), s32[]{:S(2)}) async-start(), calls=%async_computation.8 | async-start | bytes 1048576 | tf_op jit(solution)/shard_map/psum | solution.py:150
  992.6 8.8 collective-permute-start.1
  999.1 4.9 copy-start.4
  999.1 4.9 copy-start.17
  999.1 4.9 copy-start.19
  999.1 4.9 copy-start.21
  999.1 4.9 copy-start.23
  999.1 4.9 copy-start.25
  999.2 4.9 copy-start.27
Sparse Core Ops, SparseCore 0:
  989.9 308.3 all-reduce.5
  1301.2 42.1 all-reduce.3
where the time goes:
time: 1360 us; the launch traced here: 1350 us
  waiting for transfers between devices  759 us (56%)
  blocking collectives  350 us (26%)
  local copies, waits for them, and re-layouts  81.6 us (6%)
  starting transfers between devices  63.1 us (5%)
  other arithmetic  46.6 us (3%)
  matrix products  37.2 us (3%)
  between operations  15.3 us (1%)
    psum x1, waiting for transfers between devices, shards(): grad_short = lax.psum(short_local, ('dp', 'context')) * scale  289 us
    all_to_all x1, blocking collectives, inverse_rows(): lax.all_to_all(turned, 'context', split_axis=3, concat_axis=2, tiled=True)  196 us
    all_to_all x1, waiting for transfers between devices, forward_rows(): lax.all_to_all(turned, 'context', split_axis=2, concat_axis=3, tiled=True)  184 us
    all_to_all x1, blocking collectives, forward_rows(): lax.all_to_all(turned, 'context', split_axis=2, concat_axis=3, tiled=True)  103 us
    all_to_all x1, waiting for transfers between devices, inverse_rows(): lax.all_to_all(turned, 'context', split_axis=3, concat_axis=2, tiled=True)  98.5 us
    all_to_all x2, waiting for transfers between devices, inverse_rows(): lax.all_to_all(values, 'context', split_axis=1, concat_axis=2, tiled=True)  85 us
    all_to_all x1, waiting for transfers between devices, forward_rows(): lax.all_to_all(values.reshape(count, 1, block_len, width), 'context', spl...  53.7 us
    psum x1, waiting for transfers between devices, shards(): grad_long = lax.psum(dfilt_local, 'dp') * scale  43.4 us
  transfers between devices with their start and end apart: 9, of which 9 were waited for; matrix products, arithmetic and copies ran while one was open for 1% of the time, Pallas kernels for 0%

commit v1 on v0

--- a/solution.py
+++ b/solution.py
@@ -148,7 +148,7 @@
     )
     scale = 1.0 / math.sqrt(lax.axis_size("dp") * block_len * lax.axis_size("context"))
     grad_long = lax.psum(dfilt_local, "dp") * scale
-    grad_short = lax.psum(short_local, ("dp", "context")) * scale
+    grad_short = jnp.sum(lax.all_gather(short_local, ("dp", "context")), axis=0) * scale
     return (mixed, grad_inputs.astype(jnp.bfloat16)[:, None], grad_long, grad_short)
 
 

time: 1360 us -> 1240 us (0.912)
  waiting for transfers between devices: 759 us -> 632 us
    psum x1 -> x0, waiting for transfers between devices: 289 us -> none  [shards(): grad_short = lax.psum(short_local, ('dp', 'context')) * scale]
    all_gather x0 -> x1, waiting for transfers between devices: none -> 195 us  [shards(): lax.all_gather(short_local, ('dp', 'context'))]
    psum x1, waiting for transfers between devices: 43.4 us -> 9.67 us  [shards(): grad_long = lax.psum(dfilt_local, 'dp') * scale]
  transfers between devices with their start and end apart: 9 -> 9, of which waited for: 9 -> 9; matrix products, arithmetic and copies ran while one was open for 1% -> 3% of each run, Pallas kernels for 0% -> 0%
where the time goes in v1:
time: 1240 us; the launch traced here: 1230 us
  waiting for transfers between devices  632 us (51%)
  blocking collectives  350 us (28%)
  local copies, waits for them, and re-layouts  80.3 us (6%)
  starting transfers between devices  62.8 us (5%)
  other arithmetic  51.3 us (4%)
  matrix products  37.2 us (3%)
  between operations  16.7 us (1%)
    all_to_all x1, blocking collectives, inverse_rows(): lax.all_to_all(turned, 'context', split_axis=3, concat_axis=2, tiled=True)  196 us
    all_gather x1, waiting for transfers between devices, shards(): lax.all_gather(short_local, ('dp', 'context'))  195 us
    all_to_all x1, waiting for transfers between devices, forward_rows(): lax.all_to_all(turned, 'context', split_axis=2, concat_axis=3, tiled=True)  184 us
    all_to_all x1, blocking collectives, forward_rows(): lax.all_to_all(turned, 'context', split_axis=2, concat_axis=3, tiled=True)  103 us
    all_to_all x1, waiting for transfers between devices, inverse_rows(): lax.all_to_all(turned, 'context', split_axis=3, concat_axis=2, tiled=True)  98.5 us
    all_to_all x2, waiting for transfers between devices, inverse_rows(): lax.all_to_all(values, 'context', split_axis=1, concat_axis=2, tiled=True)  85.1 us
    all_to_all x1, waiting for transfers between devices, forward_rows(): lax.all_to_all(values.reshape(count, 1, block_len, width), 'context', spl...  53.7 us
    all_to_all x1, blocking collectives, forward_rows(): lax.all_to_all(values.reshape(count, 1, block_len, width), 'context', spl...  40.9 us
  transfers between devices with their start and end apart: 9, of which 9 were waited for; matrix products, arithmetic and copies ran while one was open for 3% of the time, Pallas kernels for 0%

profile of v1, /device:TPU:1, one launch (start us, length us, event | category | flops | bytes accessed | tf_op | source)
XLA Modules:
  0.0 1230.6 jit_solution(9815066965378334629)
XLA Ops:
  8.0 1.4 copy.62
  9.4 1.4 copy.63
  10.8 1.4 copy.64
  12.3 6.2 collective-permute-start
  19.1 2.1 collective-permute-done
  21.1 1.9 maximum_convert_fusion
  23.1 3.9 multiply_add_fusion
  27.0 1.4 copy-done.2
  28.4 1.8 fusion.95
  30.2 1.9 maximum_bitcast_fusion.4
  32.1 17.8 %all-to-all-start = ((f32[2,1,128,1024]{3,0,1,2:T(2,128)}), f32[2,1,128,1024]{3,0,1,2:T(2,128)S(1)}, u32[]{:S(2)}, u32[]{:S(2)}) async-start(f32[2,1,128,1024]{3,0,1,2:T(2,128)} %maximum_bitcast_fusion.4), calls=%async_computation | async-start | bytes 2097152 | tf_op jit(solution)/shard_map/all_to_all | solution.py:36
  50.3 53.7 %all-to-all-done = f32[2,1,128,1024]{3,0,1,2:T(2,128)S(1)} async-done(((f32[2,1,128,1024]{3,0,1,2:T(2,128)}), f32[2,1,128,1024]{3,0,1,2:T(2,128)S(1)}, u32[]{:S(2)}, u32[]{:S(2)}) %all-to-all-start) | async-done | bytes 1048608 | tf_op jit(solution)/shard_map/all_to_all | solution.py:36
  104.0 5.2 convolution_bitcast_fusion
  109.2 7.3 copy.67
  116.5 7.8 all-to-all-start.1
  125.6 184.3 %all-to-all-done.1 = f32[2,2,128,2,1024]{4,1,0,3,2:T(2,128)} async-done(((f32[2,2,128,2,1024]{4,1,0,3,2:T(2,128)}), f32[2,2,128,2,1024]{4,1,0,3,2:T(2,128)}, u32[]{:S(2)}, u32[]{:S(2)}) %all-to-all-start.1) | async-done | bytes 4194336 | tf_op jit(solution)/shard_map/all_to_all | solution.py:54
  309.9 5.4 copy.69
  315.4 8.1 fusion.4
  323.8 1.7 copy-done
  325.5 3.3 fusion.21
  328.8 4.2 copy.78
  333.0 10.6 all-to-all-start.2
  343.8 98.5 %all-to-all-done.2 = f32[1,2,2,128,1024]{4,1,2,0,3:T(2,128)} async-done(((f32[1,2,2,128,1024]{4,1,2,0,3:T(2,128)}), f32[1,2,2,128,1024]{4,1,2,0,3:T(2,128)}, u32[]{:S(2)}, u32[]{:S(2)}) %all-to-all-start.2) | async-done | bytes 2097184 | tf_op jit(solution)/shard_map/all_to_all | solution.py:70
  442.3 2.7 copy.79
  445.0 2.2 copy.80
  447.1 3.8 reshape.785
  450.9 3.1 fusion.30
  455.2 7.6 all-to-all-start.3
  464.0 32.8 %all-to-all-done.3 = f32[1,64,2,1024]{3,2,0,1:T(2,128)S(1)} async-done(((f32[1,64,2,1024]{3,2,0,1:T(2,128)}), f32[1,64,2,1024]{3,2,0,1:T(2,128)S(1)}, u32[]{:S(2)}, u32[]{:S(2)}) %all-to-all-start.3) | async-done | bytes 524320 | tf_op jit(solution)/shard_map/all_to_all | solution.py:78
  498.0 2.2 fusion.44
  500.1 9.3 all-reduce
  510.6 1.6 squeeze_reshape.9
  512.2 3.0 fusion.48
  515.3 40.9 %all_to_all.105 = f32[1,1,128,1024]{3,0,1,2:T(1,128)} all-to-all(f32[1,1,128,1024]{3,0,1,2:T(1,128)S(1)} %fusion.48), channel_id=1, replica_groups=mesh['dp'=2,'tensor'=4,'context'=64] {'context'}, dimensions={2} | all-to-all | bytes 1048576 | tf_op jit(solution)/shard_map/all_to_all | solution.py:36
  556.1 3.1 reduce
  559.2 2.1 reshape.786
  561.3 4.3 convolution_bitcast_fusion.1
  565.6 4.2 copy.85
  569.9 103.5 %all_to_all.106 = f32[1,2,128,2,1024]{4,1,3,0,2:T(2,128)S(1)} all-to-all(f32[1,2,128,2,1024]{4,1,3,0,2:T(2,128)} %copy.85), channel_id=1, replica_groups=mesh['dp'=2,'tensor'=4,'context'=64] {'context'}, dimensions={2} | all-to-all | bytes 4194304 | tf_op jit(solution)/shard_map/all_to_all | solution.py:54
  674.4 2.5 copy.87
  676.9 4.1 copy.88
  681.0 3.6 fusion.24
  685.5 5.0 fusion.7
  690.5 7.3 copy.94
  697.8 196.5 %all_to_all.107 = f32[2,2,2,128,1024]{4,1,0,2,3:T(2,128)S(1)} all-to-all(f32[2,2,2,128,1024]{4,1,0,2,3:T(2,128)} %copy.94), channel_id=1, replica_groups=mesh['dp'=2,'tensor'=4,'context'=64] {'context'}, dimensions={3} | all-to-all | bytes 8388608 | tf_op jit(solution)/shard_map/all_to_all | solution.py:70
  894.3 5.3 copy.96
  899.6 6.0 all_to_all.95
  905.6 4.6 fusion.28
  910.2 1.8 copy.97
  912.0 8.2 all-to-all-start.7
  920.2 1.6 squeeze_reshape.7
  921.9 52.3 %all-to-all-done.7 = f32[2,64,2,1024]{3,2,0,1:T(2,128)} async-done(((f32[2,64,2,1024]{3,2,0,1:T(2,128)}), f32[2,64,2,1024]{3,2,0,1:T(2,128)}, u32[]{:S(2)}, u32[]{:S(2)}) %all-to-all-start.7) | async-done | bytes 1048608 | tf_op jit(solution)/shard_map/all_to_all | solution.py:78
  976.7 1.6 squeeze.10
  978.3 7.8 fusion.41
  986.1 4.3 multiply_reduce_fusion
  991.3 2.6 pad_maximum_fusion.1
  993.9 4.4 collective-permute-start.1
  999.2 3.8 collective-permute-done.1
  1003.0 1.4 pad_maximum_fusion
  1004.5 3.8 fusion.40
  1009.5 9.7 all-reduce.3.cloned.1.call-done
  1019.2 1.9 broadcast_multiply_fusion
  1021.1 195.2 %all-gather.3.cloned.1.call-done = f32[384,7,1024]{2,1,0:T(8,128)} async-done(((f32[3,7,1024]{2,1,0:T(8,128)}), f32[384,7,1024]{2,1,0:T(8,128)}) %all-gather.3.cloned.1.call-update) | async-done | bytes 11010064 | tf_op jit(solution)/shard_map/all_gather | solution.py:151
  1216.2 5.8 reduce_sum.99
  (108 shorter events, 15.3 us)
Async XLA Ops:
  8.0 10.5 copy-start.26
  8.0 10.7 copy-start.11
  12.3 8.9 collective-permute-start
  18.6 4.5 copy-start.14
  18.6 4.4 copy-start.16
  18.6 4.4 copy-start.18
  18.6 4.4 copy-start.20
  18.7 4.4 copy-start.22
  18.7 4.4 copy-start.24
  27.0 1.4 copy-start.2
  32.1 71.9 %all-to-all-start = ((f32[2,1,128,1024]{3,0,1,2:T(2,128)}), f32[2,1,128,1024]{3,0,1,2:T(2,128)S(1)}, u32[]{:S(2)}, u32[]{:S(2)}) async-start(f32[2,1,128,1024]{3,0,1,2:T(2,128)} %maximum_bitcast_fusion.4), calls=%async_computation | async-start | bytes 2097152 | tf_op jit(solution)/shard_map/all_to_all | solution.py:36
  50.3 58.9 %copy-start.9 = (f32[1,128,64,2]{1,2,0,3:T(8,128)}, f32[1,128,64,2]{1,2,0,3:T(8,128)S(1)}, u32[]{:S(2)}) copy-start(f32[1,128,64,2]{1,2,0,3:T(8,128)S(1)} %get-tuple-element.55) | copy-start | bytes 196612
  50.3 58.9 %copy-start.10 = (f32[1,128,64,2]{1,2,0,3:T(8,128)}, f32[1,128,64,2]{1,2,0,3:T(8,128)S(1)}, u32[]{:S(2)}) copy-start(f32[1,128,64,2]{1,2,0,3:T(8,128)S(1)} %get-tuple-element.56) | copy-start | bytes 196612
  116.5 193.4 %all-to-all-start.1 = ((f32[2,2,128,2,1024]{4,1,0,3,2:T(2,128)}), f32[2,2,128,2,1024]{4,1,0,3,2:T(2,128)}, u32[]{:S(2)}, u32[]{:S(2)}) async-start(f32[2,2,128,2,1024]{4,1,0,3,2:T(2,128)} %copy.67), calls=%async_computation.1 | async-start | bytes 8388608 | tf_op jit(solution)/shard_map/all_to_all | solution.py:54
  124.9 190.5 %copy-start.7 = (f32[1,2,128,128]{3,2,1,0:T(8,128)}, f32[1,2,128,128]{3,2,1,0:T(8,128)S(1)}, u32[]{:S(2)}) copy-start(f32[1,2,128,128]{3,2,1,0:T(8,128)S(1)} %get-tuple-element.50) | copy-start | bytes 393220
  124.9 190.5 %copy-start.8 = (f32[1,2,128,128]{3,2,1,0:T(8,128)}, f32[1,2,128,128]{3,2,1,0:T(8,128)S(1)}, u32[]{:S(2)}) copy-start(f32[1,2,128,128]{3,2,1,0:T(8,128)S(1)} %get-tuple-element.51) | copy-start | bytes 393220
  323.5 2.0 copy-start
  333.0 109.2 %all-to-all-start.2 = ((f32[1,2,2,128,1024]{4,1,2,0,3:T(2,128)}), f32[1,2,2,128,1024]{4,1,2,0,3:T(2,128)}, u32[]{:S(2)}, u32[]{:S(2)}) async-start(f32[1,2,2,128,1024]{4,1,2,0,3:T(2,128)} %copy.78), calls=%async_computation.2 | async-start | bytes 4194304 | tf_op jit(solution)/shard_map/all_to_all | solution.py:70
  343.8 107.1 %copy-start.12 = (f32[1,64,128]{2,1,0:T(8,128)}, f32[1,64,128]{2,1,0:T(8,128)S(1)}, u32[]{:S(2)}) copy-start(f32[1,64,128]{2,1,0:T(8,128)S(1)} %get-tuple-element.68) | copy-start | bytes 98308
  450.9 11.9 copy-start.5
  455.2 41.6 %all-to-all-start.3 = ((f32[1,64,2,1024]{3,2,0,1:T(2,128)}), f32[1,64,2,1024]{3,2,0,1:T(2,128)S(1)}, u32[]{:S(2)}, u32[]{:S(2)}) async-start(f32[1,64,2,1024]{3,2,0,1:T(2,128)} %copy.81), calls=%async_computation.3 | async-start | bytes 1048576 | tf_op jit(solution)/shard_map/all_to_all | solution.py:78
  681.0 3.7 copy-start.1
  899.6 6.0 copy-start.13
  912.0 62.2 %all-to-all-start.7 = ((f32[2,64,2,1024]{3,2,0,1:T(2,128)}), f32[2,64,2,1024]{3,2,0,1:T(2,128)}, u32[]{:S(2)}, u32[]{:S(2)}) async-start(f32[2,64,2,1024]{3,2,0,1:T(2,128)} %copy.97), calls=%async_computation.7 | async-start | bytes 2097152 | tf_op jit(solution)/shard_map/all_to_all | solution.py:78
  920.2 99.0 %all-reduce.3.cloned.1.call-start = ((), (), s32[]{:S(2)}) async-start(), calls=%async_computation.8 | async-start | bytes 1048576 | tf_op jit(solution)/shard_map/psum | solution.py:150
  921.8 56.4 %copy-start.27 = (f32[1024]{0:T(1024)S(1)}, f32[1024]{0:T(1024)}, u32[]{:S(2)}) copy-start(f32[1024]{0:T(1024)} %param.12) | copy-start | bytes 12292
  921.8 56.4 %copy-start.28 = (f32[128]{0:T(128)S(1)}, f32[128]{0:T(128)}, u32[]{:S(2)}) copy-start(f32[128]{0:T(128)} %get-tuple-element.22) | copy-start | bytes 1540
  921.8 56.4 %copy-start.29 = (f32[128]{0:T(128)S(1)}, f32[128]{0:T(128)}, u32[]{:S(2)}) copy-start(f32[128]{0:T(128)} %get-tuple-element.57) | copy-start | bytes 1540
  921.8 56.4 %copy-start.30 = (f32[128]{0:T(128)S(1)}, f32[128]{0:T(128)}, u32[]{:S(2)}) copy-start(f32[128]{0:T(128)} %get-tuple-element.58) | copy-start | bytes 1540
  976.6 239.6 %all-gather.3.cloned.1.call-start = ((), (), s32[]{:S(2)}) async-start(), calls=%async_computation.9 | async-start | bytes 12681216 | tf_op jit(solution)/shard_map/all_gather | solution.py:151
  986.1 4.3 copy-start.3
  990.4 8.0 copy-start.6
  991.3 11.7 copy-start.4
  993.9 9.1 collective-permute-start.1
  999.2 5.3 copy-start.15
  999.2 5.3 copy-start.17
  999.2 5.3 copy-start.19
  999.2 5.3 copy-start.21
  999.2 5.3 copy-start.23
  999.2 5.3 copy-start.25
Sparse Core Ops, SparseCore 0:
  976.7 42.4 all-reduce.2
Sparse Core Ops, SparseCore 1:
  991.4 224.7 all-gather.2
